TPU v7x, 32 devices: a whole 2x2x4 slice. The times are simulated.
32 devices in a mesh: row: 8 (over y, x, core), col: 4 (over z).
Axes of the slice: x: 2, y: 2, z: 4, core: 2. Of those that a mesh axis runs over, the one named last changes fastest.
Arguments:
- positions: float32 [3, 32768], P(None, ('row', 'col')), may hold values from 0 to 1
- segments: float32 [3, 32768], P(None, ('row', 'col')), may hold values from -1.2 to 1.2
- radius: float32 [32768], P(('row', 'col')), may hold values from 0.05 to 0.2
- currents: float32 [2, 32768], P(None, ('row', 'col')), may hold values from -6 to 6
- resist: float32 [32768], P(('row', 'col')), may hold values from 0.3 to 3
- slot_of: int32 [32768], P(('row', 'col')), may hold values from 0 to 1023, as said below
- pair_list: int32 [1024, 2], P(('row', 'col')), may hold values from 0 to 63, as said below
- near_flag: int32 [1024], P(('row', 'col')), may hold values from 0 to 2, as said below
Outputs:
- voltage: float32 [2, 32768], P(None, ('row', 'col'))
Inputs may be any that keep to these rules, and one draw needn't show every extreme that they name: `slot_of`: the elements of shard d hold the values 0 to 1023 once each; a value s puts the element in cluster d * 2 + s // 512. `pair_list`: shard d = r * 4 + c lists 32 slots; each live slot holds a pair (I, J) with I <= J, I in clusters r * 2 * 4 to (r + 1) * 2 * 4 - 1 and (J // 2) % 4 = c; a pair stands in one live slot at most, over all shards. Empty slots hold I = r * 2 * 4 and J = c * 2. `near_flag`: 0 marks an empty slot.
All inputs are finite; a program needn't handle non-finite values.
Results may differ from a plain program's by a relative error of at most 0.0003.
Values sent between devices are 32-bit elements; how exact they have to be, the bound alone decides.
A program may use at most 64 MiB of HBM per device.

v0:
```python
import math
import jax
import jax.numpy as jnp
from jax import lax
from jax.sharding import PartitionSpec as P

CS = 512
gauss_step = 0.5 / math.sqrt(3.0)
kernel_gain = 0.25
group_size = 4


def partner(block, axis, distance):
    count = lax.axis_size(axis)
    route = []
    for low in range(count):
        high = low | 1 << distance
        if high != low and high < count:
            route += [(low, high), (high, low)]
    return lax.ppermute(block, axis, route)


def tile_block(
    points_first, vectors_first, radii_first, points_second, vectors_second, radii_second, is_near
):
    softening = radii_first[:, None] ** 2 + radii_second[None, :] ** 2
    alignment = vectors_first[0][:, None] * vectors_second[0][None, :]
    for component in (1, 2):
        alignment = (
            alignment + vectors_first[component][:, None] * vectors_second[component][None, :]
        )

    def far_part():
        squared = softening
        for component in range(3):
            squared = (
                squared
                + (points_first[component][:, None] - points_second[component][None, :]) ** 2
            )
        return 1.0 / jnp.sqrt(squared)

    def near_part():
        summed = jnp.zeros_like(softening)
        for sign_first in (-1.0, 1.0):
            for sign_second in (-1.0, 1.0):
                squared = softening
                for component in range(3):
                    moved_first = (
                        points_first[component] + sign_first * gauss_step * vectors_first[component]
                    )
                    moved_second = (
                        points_second[component]
                        + sign_second * gauss_step * vectors_second[component]
                    )
                    squared = squared + (moved_first[:, None] - moved_second[None, :]) ** 2
                summed = summed + 1.0 / jnp.sqrt(squared)
        return 0.25 * summed

    inverse = lax.cond(is_near, near_part, far_part)
    return kernel_gain * alignment * inverse


def slot_terms(block_first, block_second, flag_value, diagonal_pair):
    step_rows = min(128, CS)

    def live_terms():
        is_near = flag_value == 2
        rows_out = []
        mirror_sum = jnp.zeros((2, CS), jnp.float32)
        for offset in range(0, CS, step_rows):
            portion = block_first[:, offset : offset + step_rows]
            kernel_tile = tile_block(
                portion[0:3],
                portion[3:6],
                portion[6],
                block_second[0:3],
                block_second[3:6],
                block_second[6],
                is_near,
            )
            rows_out.append(
                jnp.dot(block_second[7:9], kernel_tile.T, precision=lax.Precision.HIGHEST)
            )
            mirror_sum = mirror_sum + jnp.dot(
                portion[7:9], kernel_tile, precision=lax.Precision.HIGHEST
            )
        mirror_weight = 1.0 - diagonal_pair.astype(jnp.float32)
        return (jnp.concatenate(rows_out, 1), mirror_weight * mirror_sum)

    def empty_terms():
        blank = jnp.zeros((2, CS), jnp.float32)
        return (blank, blank)

    return lax.cond(flag_value > 0, live_terms, empty_terms)


def on_device(positions, segments, radius, currents, resist, slot_of, pair_list, near_flag):
    local_count = positions.shape[1]
    packed = jnp.concatenate([positions, segments, radius[None, :], currents], 0)
    ordered = jnp.zeros_like(packed).at[:, slot_of].set(packed)
    row_block = lax.all_gather(ordered, "col", axis=1, tiled=True)
    col_block = lax.all_gather(ordered, "row", axis=1, tiled=True)
    col_count = lax.axis_size("col")
    row_count = lax.axis_size("row")
    row_pos = lax.axis_index("row")
    per_device = local_count // CS
    row_span = per_device * col_count
    col_span = per_device * row_count
    slot_count = pair_list.shape[0]
    local_first = pair_list[:, 0] - row_pos * row_span
    local_second = pair_list[:, 1] // row_span * per_device + pair_list[:, 1] % per_device
    diagonal_all = (pair_list[:, 0] == pair_list[:, 1]).astype(jnp.int32)

    def add_terms(sums_pair, slot_index, direct_part, mirror_part):
        row_sum, col_sum = sums_pair
        first_id = local_first[slot_index]
        second_id = local_second[slot_index]
        current = lax.dynamic_slice_in_dim(row_sum, first_id * CS, CS, 1)
        row_sum = lax.dynamic_update_slice_in_dim(row_sum, current + direct_part, first_id * CS, 1)
        current = lax.dynamic_slice_in_dim(col_sum, second_id * CS, CS, 1)
        col_sum = lax.dynamic_update_slice_in_dim(col_sum, current + mirror_part, second_id * CS, 1)
        return (row_sum, col_sum)

    row_start = jnp.zeros((2, row_span * CS), jnp.float32)
    col_start = jnp.zeros((2, col_span * CS), jnp.float32)
    half_count = slot_count // 2

    def visit_group(group_index, sums_now):
        for inner in range(group_size):
            slot_index = group_index * group_size + inner
            block_first = lax.dynamic_slice_in_dim(row_block, local_first[slot_index] * CS, CS, 1)
            block_second = lax.dynamic_slice_in_dim(col_block, local_second[slot_index] * CS, CS, 1)
            direct_part, mirror_part = slot_terms(
                block_first, block_second, near_flag[slot_index], diagonal_all[slot_index] > 0
            )
            sums_now = add_terms(sums_now, slot_index, direct_part, mirror_part)
        return sums_now

    row_sum, col_sum = lax.fori_loop(
        0, half_count // group_size, visit_group, (row_start, col_start)
    )
    row_tiles = row_block.reshape(9, row_span, CS)
    col_tiles = col_block.reshape(9, col_span, CS)
    lent_first = jnp.take(row_tiles, local_first[half_count:], axis=1)
    lent_second = jnp.take(col_tiles, local_second[half_count:], axis=1)
    lent_blocks = jnp.concatenate([lent_first, lent_second], 0)
    lent_codes = (near_flag[half_count:] + 3 * diagonal_all[half_count:]).astype(jnp.float32)
    top_bit = lax.axis_size("row").bit_length() - 2
    borrowed_blocks, borrowed_codes = partner((lent_blocks, lent_codes), "row", top_bit)

    def help_group(group_index, results):
        for inner in range(group_size):
            item = group_index * group_size + inner
            block_pair = lax.dynamic_index_in_dim(borrowed_blocks, item, 1, keepdims=False)
            code_value = borrowed_codes[item].astype(jnp.int32)
            direct_part, mirror_part = slot_terms(
                block_pair[0:9], block_pair[9:18], code_value % 3, code_value // 3 > 0
            )
            both_parts = jnp.stack([direct_part, mirror_part])[:, :, None, :]
            results = lax.dynamic_update_slice(results, both_parts, (0, 0, item, 0))
        return results

    helped = lax.fori_loop(
        0, half_count // group_size, help_group, jnp.zeros((2, 2, half_count, CS), jnp.float32)
    )
    returned = partner(helped, "row", top_bit)
    row_sum = (
        row_sum.reshape(2, row_span, CS)
        .at[:, local_first[half_count:], :]
        .add(returned[0])
        .reshape(2, row_span * CS)
    )
    col_sum = (
        col_sum.reshape(2, col_span, CS)
        .at[:, local_second[half_count:], :]
        .add(returned[1])
        .reshape(2, col_span * CS)
    )
    owned = lax.psum_scatter(row_sum, "col", scatter_dimension=1, tiled=True) + lax.psum_scatter(
        col_sum, "row", scatter_dimension=1, tiled=True
    )
    induced = owned[:, slot_of]
    voltage_real = resist * currents[0] - induced[1]
    voltage_imag = resist * currents[1] + induced[0]
    return jnp.stack([voltage_real, voltage_imag])


def solution(mesh):
    return jax.shard_map(
        on_device,
        mesh=mesh,
        in_specs=(
            P(None, ("row", "col")),
            P(None, ("row", "col")),
            P(("row", "col")),
            P(None, ("row", "col")),
            P(("row", "col")),
            P(("row", "col")),
            P(("row", "col"), None),
            P(("row", "col")),
        ),
        out_specs=P(None, ("row", "col")),
        check_vma=False,
    )
```

profile of v0, /device:TPU:0, one launch (start us, length us, event | category | flops | bytes accessed | tf_op | source)
XLA Modules:
  0.0 470.7 jit_solution(10847752534651488676)
XLA Ops:
  6.5 0.7 broadcast_clamp_fusion
  7.2 0.8 maximum_bitcast_fusion.8
  8.3 3.2 scatter_custom_fusion
  11.5 39.7 %all_gather.7 = f32[9,4096]{0,1:T(8,128)S(1)} all-gather(f32[9,1024]{0,1:T(8,128)S(1)} %scatter_custom_fusion), channel_id=1, replica_groups=mesh['row'=8,'col'=4] {'col'}, dimensions={1}, use_global_device_ids=true | all-gather | bytes 184320 | tf_op jit(solution)/shard_map/all_gather | solution.py:101
  51.2 24.6 %all_gather.6 = f32[9,8192]{0,1:T(8,128)} all-gather(f32[9,1024]{0,1:T(8,128)S(1)} %scatter_custom_fusion), channel_id=1, replica_groups=mesh['row'=8,'col'=4] {'row'}, dimensions={1}, use_global_device_ids=true | all-gather | bytes 331776 | tf_op jit(solution)/shard_map/all_gather | solution.py:102
  76.6 2.9 copy.23
  80.0 1.4 gather_fusion.1
  81.5 1.2 select_bitcast_fusion
  83.3 2.0 collective-permute-start
  85.9 2.9 copy.20
  88.8 10.1 %collective-permute-done.1 = f32[18,16,512]{2,1,0:T(8,128)} collective-permute-done((f32[18,16,512]{2,1,0:T(8,128)S(1)}, f32[18,16,512]{2,1,0:T(8,128)}, u32[]{:S(2)}, u32[]{:S(2)}) %collective-permute-start.1) | collective-permute-done | bytes 589856 | tf_op jit(solution)/shard_map/ppermute | solution.py:20
  98.9 1.4 copy.25
  100.4 50.1 %while.34 = (s32[]{:T(128)}, f32[2,2,16,512]{3,1,0,2:T(2,128)S(1)}, f32[16]{0:T(128)S(1)}, f32[18,16,512]{2,0,1:T(8,128)S(1)}, s32[]{:T(128)}, /*index=5*/s32[]{...) while((s32[]{:T(128)}, f32[2,2,16,512]{3,1,0,2:T(2,128)S(1)}, ...), condition=%wide.region_84.85_spmd, body=%wide.region_43.84_spmd.sunk | while | flops 108167224 | bytes 22711308 | solution.py:163
  100.6 0.7 fusion.711
  104.0 4.5 conditional.54
  108.5 4.5 conditional.53
  113.1 0.7 fusion.711
  116.4 4.4 conditional.55
  120.9 4.5 conditional.53
  125.4 4.5 conditional.52
  130.0 0.7 fusion.711
  133.3 4.4 conditional.55
  138.0 0.7 fusion.711
  141.4 4.4 conditional.55
  145.9 4.5 conditional.52
  150.5 39.8 %collective-permute-start.2 = (f32[2,2,16,512]{3,1,0,2:T(2,128)S(1)}, f32[2,2,16,512]{3,1,0,2:T(2,128)S(1)}, u32[]{:S(2)}, u32[]{:S(2)}) collective-permute-start(f32[2,2,16,512]{3,1,0,2:T(2,128)S(1)} %get-tuple-element.1886), channel_id=1, source_target_pairs={{0,16},{16,0},{4,20},{20,4},{8,24},{24,8},{12,28},{28,12},{1,17},{... | collective-permute-start | bytes 393224 | tf_op jit(solution)/shard_map/ppermute | solution.py:20
  190.4 168.9 %while.33 = (s32[]{:T(128)}, f32[2,4096]{1,0:T(2,128)S(1)}, f32[2,8192]{1,0:T(2,128)S(1)}, s32[32]{0:T(128)S(1)}, s32[32]{0:T(128)S(1)}, /*index=5*/s32[32]{0:T(...) while((s32[]{:T(128)}, f32[2,4096]{1,0:T(2,128)S(1)}, ...), condition=%wide.region_42.43_spmd, body=%wide.region_1.42_spmd.sunk | while | flops 108167248 | bytes 22744584 | solution.py:139
  204.6 0.7 fusion.708
  207.7 0.7 fusion.709
  214.1 6.7 %conditional.51 = (f32[2,512]{1,0:T(2,128)S(1)}, f32[2,512]{1,0:T(2,128)S(1)}) conditional(s32[]{:T(128)} %convert_element_type.265, () %tuple.1090, (f32[9,8192]{1,0:T(8,128)S(1)}, s32[]{:T(128)}, f32[9,4096]{1,0:T(8,128)S(1)}, s32[]{:T(128)}, s32[]{:T(128)}, /*index=5*/s32[32]{0:T(128)S(1)}, s32[]{:T(128)}) %tuple.1091), branch_computations={%region_32.32_spmd, %region_33.41_spmd} | conditional | flops 27039756 | bytes 5661272 | solution.py:94
  220.8 6.8 %conditional.50 = (f32[2,512]{1,0:T(2,128)S(1)}, f32[2,512]{1,0:T(2,128)S(1)}) conditional(s32[]{:T(128)} %convert_element_type.264, () %tuple.1088, (f32[9,8192]{1,0:T(8,128)S(1)}, s32[]{:T(128)}, f32[9,4096]{1,0:T(8,128)S(1)}, s32[]{:T(128)}, s32[]{:T(128)}, /*index=5*/s32[32]{0:T(128)S(1)}, s32[]{:T(128)}) %tuple.1089), branch_computations={%region_22.22_spmd, %region_23.31_spmd} | conditional | flops 27039756 | bytes 5661272 | solution.py:94
  221.5 0.7 dynamic_slice.409
  227.6 6.8 %conditional.49 = (f32[2,512]{1,0:T(2,128)S(1)}, f32[2,512]{1,0:T(2,128)S(1)}) conditional(s32[]{:T(128)} %convert_element_type.263, () %tuple.1086, (f32[9,8192]{1,0:T(8,128)S(1)}, s32[]{:T(128)}, f32[9,4096]{1,0:T(8,128)S(1)}, s32[]{:T(128)}, s32[]{:T(128)}, /*index=5*/s32[32]{0:T(128)S(1)}, s32[]{:T(128)}) %tuple.1087), branch_computations={%region_12.12_spmd, %region_13.21_spmd} | conditional | flops 27039756 | bytes 5661272 | solution.py:94
  234.4 8.2 %conditional.48 = (f32[2,512]{1,0:T(2,128)S(1)}, f32[2,512]{1,0:T(2,128)S(1)}) conditional(s32[]{:T(128)} %convert_element_type.262, () %tuple.1084, (f32[9,8192]{1,0:T(8,128)S(1)}, s32[]{:T(128)}, f32[9,4096]{1,0:T(8,128)S(1)}, s32[]{:T(128)}, s32[]{:T(128)}, /*index=5*/s32[32]{0:T(128)S(1)}, s32[]{:T(128)}) %tuple.1085), branch_computations={%region_2.2_spmd, %region_3.11_spmd} | conditional | flops 27039756 | bytes 5661272 | solution.py:94
  242.9 0.7 fusion.708
  246.0 0.7 fusion.709
  252.4 8.1 %conditional.51 = (f32[2,512]{1,0:T(2,128)S(1)}, f32[2,512]{1,0:T(2,128)S(1)}) conditional(s32[]{:T(128)} %convert_element_type.265, () %tuple.1090, (f32[9,8192]{1,0:T(8,128)S(1)}, s32[]{:T(128)}, f32[9,4096]{1,0:T(8,128)S(1)}, s32[]{:T(128)}, s32[]{:T(128)}, /*index=5*/s32[32]{0:T(128)S(1)}, s32[]{:T(128)}) %tuple.1091), branch_computations={%region_32.32_spmd, %region_33.41_spmd} | conditional | flops 27039756 | bytes 5661272 | solution.py:94
  260.5 6.8 %conditional.50 = (f32[2,512]{1,0:T(2,128)S(1)}, f32[2,512]{1,0:T(2,128)S(1)}) conditional(s32[]{:T(128)} %convert_element_type.264, () %tuple.1088, (f32[9,8192]{1,0:T(8,128)S(1)}, s32[]{:T(128)}, f32[9,4096]{1,0:T(8,128)S(1)}, s32[]{:T(128)}, s32[]{:T(128)}, /*index=5*/s32[32]{0:T(128)S(1)}, s32[]{:T(128)}) %tuple.1089), branch_computations={%region_22.22_spmd, %region_23.31_spmd} | conditional | flops 27039756 | bytes 5661272 | solution.py:94
  261.2 0.7 dynamic_slice.409
  267.3 6.8 %conditional.49 = (f32[2,512]{1,0:T(2,128)S(1)}, f32[2,512]{1,0:T(2,128)S(1)}) conditional(s32[]{:T(128)} %convert_element_type.263, () %tuple.1086, (f32[9,8192]{1,0:T(8,128)S(1)}, s32[]{:T(128)}, f32[9,4096]{1,0:T(8,128)S(1)}, s32[]{:T(128)}, s32[]{:T(128)}, /*index=5*/s32[32]{0:T(128)S(1)}, s32[]{:T(128)}) %tuple.1087), branch_computations={%region_12.12_spmd, %region_13.21_spmd} | conditional | flops 27039756 | bytes 5661272 | solution.py:94
  274.1 8.2 %conditional.48 = (f32[2,512]{1,0:T(2,128)S(1)}, f32[2,512]{1,0:T(2,128)S(1)}) conditional(s32[]{:T(128)} %convert_element_type.262, () %tuple.1084, (f32[9,8192]{1,0:T(8,128)S(1)}, s32[]{:T(128)}, f32[9,4096]{1,0:T(8,128)S(1)}, s32[]{:T(128)}, s32[]{:T(128)}, /*index=5*/s32[32]{0:T(128)S(1)}, s32[]{:T(128)}) %tuple.1085), branch_computations={%region_2.2_spmd, %region_3.11_spmd} | conditional | flops 27039756 | bytes 5661272 | solution.py:94
  282.5 0.7 fusion.708
  285.7 0.7 fusion.709
  292.1 8.1 %conditional.51 = (f32[2,512]{1,0:T(2,128)S(1)}, f32[2,512]{1,0:T(2,128)S(1)}) conditional(s32[]{:T(128)} %convert_element_type.265, () %tuple.1090, (f32[9,8192]{1,0:T(8,128)S(1)}, s32[]{:T(128)}, f32[9,4096]{1,0:T(8,128)S(1)}, s32[]{:T(128)}, s32[]{:T(128)}, /*index=5*/s32[32]{0:T(128)S(1)}, s32[]{:T(128)}) %tuple.1091), branch_computations={%region_32.32_spmd, %region_33.41_spmd} | conditional | flops 27039756 | bytes 5661272 | solution.py:94
  300.2 6.8 %conditional.50 = (f32[2,512]{1,0:T(2,128)S(1)}, f32[2,512]{1,0:T(2,128)S(1)}) conditional(s32[]{:T(128)} %convert_element_type.264, () %tuple.1088, (f32[9,8192]{1,0:T(8,128)S(1)}, s32[]{:T(128)}, f32[9,4096]{1,0:T(8,128)S(1)}, s32[]{:T(128)}, s32[]{:T(128)}, /*index=5*/s32[32]{0:T(128)S(1)}, s32[]{:T(128)}) %tuple.1089), branch_computations={%region_22.22_spmd, %region_23.31_spmd} | conditional | flops 27039756 | bytes 5661272 | solution.py:94
  300.8 0.7 dynamic_slice.409
  307.0 6.8 %conditional.49 = (f32[2,512]{1,0:T(2,128)S(1)}, f32[2,512]{1,0:T(2,128)S(1)}) conditional(s32[]{:T(128)} %convert_element_type.263, () %tuple.1086, (f32[9,8192]{1,0:T(8,128)S(1)}, s32[]{:T(128)}, f32[9,4096]{1,0:T(8,128)S(1)}, s32[]{:T(128)}, s32[]{:T(128)}, /*index=5*/s32[32]{0:T(128)S(1)}, s32[]{:T(128)}) %tuple.1087), branch_computations={%region_12.12_spmd, %region_13.21_spmd} | conditional | flops 27039756 | bytes 5661272 | solution.py:94
  313.8 8.2 %conditional.48 = (f32[2,512]{1,0:T(2,128)S(1)}, f32[2,512]{1,0:T(2,128)S(1)}) conditional(s32[]{:T(128)} %convert_element_type.262, () %tuple.1084, (f32[9,8192]{1,0:T(8,128)S(1)}, s32[]{:T(128)}, f32[9,4096]{1,0:T(8,128)S(1)}, s32[]{:T(128)}, s32[]{:T(128)}, /*index=5*/s32[32]{0:T(128)S(1)}, s32[]{:T(128)}) %tuple.1085), branch_computations={%region_2.2_spmd, %region_3.11_spmd} | conditional | flops 27039756 | bytes 5661272 | solution.py:94
  322.2 0.7 fusion.708
  325.4 0.7 fusion.709
  331.7 6.7 %conditional.51 = (f32[2,512]{1,0:T(2,128)S(1)}, f32[2,512]{1,0:T(2,128)S(1)}) conditional(s32[]{:T(128)} %convert_element_type.265, () %tuple.1090, (f32[9,8192]{1,0:T(8,128)S(1)}, s32[]{:T(128)}, f32[9,4096]{1,0:T(8,128)S(1)}, s32[]{:T(128)}, s32[]{:T(128)}, /*index=5*/s32[32]{0:T(128)S(1)}, s32[]{:T(128)}) %tuple.1091), branch_computations={%region_32.32_spmd, %region_33.41_spmd} | conditional | flops 27039756 | bytes 5661272 | solution.py:94
  338.5 6.8 %conditional.50 = (f32[2,512]{1,0:T(2,128)S(1)}, f32[2,512]{1,0:T(2,128)S(1)}) conditional(s32[]{:T(128)} %convert_element_type.264, () %tuple.1088, (f32[9,8192]{1,0:T(8,128)S(1)}, s32[]{:T(128)}, f32[9,4096]{1,0:T(8,128)S(1)}, s32[]{:T(128)}, s32[]{:T(128)}, /*index=5*/s32[32]{0:T(128)S(1)}, s32[]{:T(128)}) %tuple.1089), branch_computations={%region_22.22_spmd, %region_23.31_spmd} | conditional | flops 27039756 | bytes 5661272 | solution.py:94
  339.1 0.7 dynamic_slice.409
  345.3 6.8 %conditional.49 = (f32[2,512]{1,0:T(2,128)S(1)}, f32[2,512]{1,0:T(2,128)S(1)}) conditional(s32[]{:T(128)} %convert_element_type.263, () %tuple.1086, (f32[9,8192]{1,0:T(8,128)S(1)}, s32[]{:T(128)}, f32[9,4096]{1,0:T(8,128)S(1)}, s32[]{:T(128)}, s32[]{:T(128)}, /*index=5*/s32[32]{0:T(128)S(1)}, s32[]{:T(128)}) %tuple.1087), branch_computations={%region_12.12_spmd, %region_13.21_spmd} | conditional | flops 27039756 | bytes 5661272 | solution.py:94
  352.1 6.8 %conditional.48 = (f32[2,512]{1,0:T(2,128)S(1)}, f32[2,512]{1,0:T(2,128)S(1)}) conditional(s32[]{:T(128)} %convert_element_type.262, () %tuple.1084, (f32[9,8192]{1,0:T(8,128)S(1)}, s32[]{:T(128)}, f32[9,4096]{1,0:T(8,128)S(1)}, s32[]{:T(128)}, s32[]{:T(128)}, /*index=5*/s32[32]{0:T(128)S(1)}, s32[]{:T(128)}) %tuple.1085), branch_computations={%region_2.2_spmd, %region_3.11_spmd} | conditional | flops 27039756 | bytes 5661272 | solution.py:94
  352.8 0.7 dynamic_slice.403
  359.3 1.2 scatter_fusion
  360.5 2.0 copy.26
  362.6 1.2 scatter_fusion.1
  363.8 2.7 copy.27
  366.6 38.1 %reduce-scatter.3.cloned.1.call-done = f32[2,1024]{0,1:T(8,128)} async-done(((f32[2,4096]{0,1:T(8,128)}), f32[2,1024]{0,1:T(8,128)}) %reduce-scatter.3.cloned.1.call-update) | async-done | bytes 8208 | tf_op jit(solution)/shard_map/reduce_scatter | solution.py:179
  404.7 53.7 %reduce-scatter.5.cloned.1.call-done = f32[2,1024]{0,1:T(8,128)} async-done(((f32[2,8192]{0,1:T(8,128)}), f32[2,1024]{0,1:T(8,128)}) %reduce-scatter.5.cloned.1.call-update) | async-done | bytes 8208 | tf_op jit(solution)/shard_map/reduce_scatter | solution.py:179
  458.5 1.3 add.6301
  459.7 2.8 gather_fusion.2
  (863 shorter events, 155.5 us)
Async XLA Ops:
  6.5 398.2 %reduce-scatter.3.cloned.1.call-start = ((), (), s32[]{:S(2)}) async-start(), calls=%async_computation.2 | async-start | bytes 2621440 | tf_op jit(solution)/shard_map/reduce_scatter | solution.py:179
  8.0 67.7 %copy-start.3 = (s32[32,2]{0,1:T(2,128)S(1)}, s32[32,2]{0,1:T(2,128)}, u32[]{:S(2)}) copy-start(s32[32,2]{0,1:T(2,128)} %param.98) | copy-start | bytes 772
  79.4 3.8 copy-start
  83.1 15.8 %collective-permute-start.1 = (f32[18,16,512]{2,1,0:T(8,128)S(1)}, f32[18,16,512]{2,1,0:T(8,128)}, u32[]{:S(2)}, u32[]{:S(2)}) collective-permute-start(f32[18,16,512]{2,1,0:T(8,128)S(1)} %copy.24), channel_id=1, source_target_pairs={{0,16},{16,0},{4,20},{20,4},{8,24},{24,8},{12,28},{28,12},{1,17},{... | collective-permute-start | bytes 1769480 | tf_op jit(solution)/shard_map/ppermute | solution.py:20
  83.3 17.0 %collective-permute-start = (f32[16]{0:T(128)S(1)}, f32[16]{0:T(128)S(1)}, u32[]{:S(2)}, u32[]{:S(2)}) collective-permute-start(f32[16]{0:T(128)S(1)} %add_convert_fusion), channel_id=1, source_target_pairs={{0,16},{16,0},{4,20},{20,4},{8,24},{24,8},{12,28},{28,12},{1,17},{... | collective-permute-start | bytes 200 | tf_op jit(solution)/shard_map/ppermute | solution.py:20
  150.5 208.8 %collective-permute-start.2 = (f32[2,2,16,512]{3,1,0,2:T(2,128)S(1)}, f32[2,2,16,512]{3,1,0,2:T(2,128)S(1)}, u32[]{:S(2)}, u32[]{:S(2)}) collective-permute-start(f32[2,2,16,512]{3,1,0,2:T(2,128)S(1)} %get-tuple-element.1886), channel_id=1, source_target_pairs={{0,16},{16,0},{4,20},{20,4},{8,24},{24,8},{12,28},{28,12},{1,17},{... | collective-permute-start | bytes 393224 | tf_op jit(solution)/shard_map/ppermute | solution.py:20
  362.6 95.9 %reduce-scatter.5.cloned.1.call-start = ((), (), s32[]{:S(2)}) async-start(), calls=%async_computation.3 | async-start | bytes 4718592 | tf_op jit(solution)/shard_map/reduce_scatter | solution.py:179
  363.8 2.8 copy-start.1
  366.6 96.5 %copy-start.2 = (f32[1024]{0:T(1024)S(1)}, f32[1024]{0:T(1024)}, u32[]{:S(2)}) copy-start(f32[1024]{0:T(1024)} %param.96) | copy-start | bytes 12292
Sparse Core Ops, SparseCore 0:
  362.7 41.9 reduce-scatter.2
  408.1 50.3 reduce-scatter.4
where the time goes:
time: 476 us; the launch traced here: 471 us
  waiting for transfers between devices  102 us (21%)
  loops' own time  83.9 us (18%)
  matrix products  77.9 us (16%)
  blocking collectives  64.3 us (14%)
  local copies, waits for them, and re-layouts  48.4 us (10%)
  starting transfers between devices  41.9 us (9%)
  other arithmetic  38.4 us (8%)
  between operations  13.9 us (3%)
    reduce_scatter x1, waiting for transfers between devices, on_device(): lax.psum_scatter(col_sum, 'row', scatter_dimension=1, tiled=True)  53.7 us
    another operation x1, loops' own time, on_device(): lax.fori_loop(0, half_count // group_size, visit_group, (row_start, col_s...  45 us
    ppermute x3, starting transfers between devices, partner(): return lax.ppermute(block, axis, route)  41.9 us
    dot_general x96, matrix products, live_terms(): jnp.dot(block_second[7:9], kernel_tile.T, precision=lax.Precision.HIGHEST)  40.9 us
    all_gather x1, blocking collectives, on_device(): row_block = lax.all_gather(ordered, 'col', axis=1, tiled=True)  39.7 us
    reduce_scatter x1, waiting for transfers between devices, on_device(): lax.psum_scatter(row_sum, 'col', scatter_dimension=1, tiled=True)  38.1 us
    dot_general x96, matrix products, live_terms(): jnp.dot(portion[7:9], kernel_tile, precision=lax.Precision.HIGHEST)  37 us
    all_gather x1, blocking collectives, on_device(): col_block = lax.all_gather(ordered, 'row', axis=1, tiled=True)  24.6 us
  transfers between devices with their start and end apart: 5, of which 3 were waited for; matrix products, arithmetic and copies ran while one was open for 23% of the time, Pallas kernels for 0%

commit v1 on v0

--- a/solution.py
+++ b/solution.py
@@ -99,7 +99,15 @@
     packed = jnp.concatenate([positions, segments, radius[None, :], currents], 0)
     ordered = jnp.zeros_like(packed).at[:, slot_of].set(packed)
     row_block = lax.all_gather(ordered, "col", axis=1, tiled=True)
-    col_block = lax.all_gather(ordered, "row", axis=1, tiled=True)
+    ways, here = (lax.axis_size("row"), lax.axis_index("row"))
+    grown, reach = (ordered, 1)
+    while reach < ways:
+        theirs = lax.ppermute(grown, "row", [(d, d ^ reach) for d in range(ways)])
+        mine_first = jnp.concatenate([grown, theirs], axis=1)
+        theirs_first = jnp.concatenate([theirs, grown], axis=1)
+        grown = jnp.where(here & reach == 0, mine_first, theirs_first)
+        reach = 2 * reach
+    col_block = grown
     col_count = lax.axis_size("col")
     row_count = lax.axis_size("row")
     row_pos = lax.axis_index("row")

time: 476 us -> 460 us (0.966)
  blocking collectives: 64.3 us -> 38.5 us
  waiting for transfers between devices: 102 us -> 112 us
    all_gather x1 -> x0, blocking collectives: 24.6 us -> none  [on_device(): col_block = lax.all_gather(ordered, 'row', axis=1, tiled=True)]
    ppermute x0 -> x3, waiting for transfers between devices: none -> 8.39 us  [on_device(): theirs = lax.ppermute(grown, 'row', [(d, d ^ reach) for d in range(ways)])]
  transfers between devices with their start and end apart: 5 -> 8, of which waited for: 3 -> 5; matrix products, arithmetic and copies ran while one was open for 23% -> 25% of each run, Pallas kernels for 0% -> 0%
where the time goes in v1:
time: 460 us; the launch traced here: 455 us
  waiting for transfers between devices  112 us (24%)
  loops' own time  82.1 us (18%)
  matrix products  76.5 us (17%)
  starting transfers between devices  45.4 us (10%)
  local copies, waits for them, and re-layouts  44.5 us (10%)
  other arithmetic  41.8 us (9%)
  blocking collectives  38.5 us (8%)
  between operations  14 us (3%)
    reduce_scatter x1, waiting for transfers between devices, on_device(): lax.psum_scatter(col_sum, 'row', scatter_dimension=1, tiled=True)  53.8 us
    another operation x1, loops' own time, on_device(): lax.fori_loop(0, half_count // group_size, visit_group, (row_start, col_s...  44.3 us
    ppermute x3, starting transfers between devices, partner(): return lax.ppermute(block, axis, route)  42.6 us
    dot_general x96, matrix products, live_terms(): jnp.dot(block_second[7:9], kernel_tile.T, precision=lax.Precision.HIGHEST)  41 us
    all_gather x1, blocking collectives, on_device(): row_block = lax.all_gather(ordered, 'col', axis=1, tiled=True)  38.5 us
    reduce_scatter x1, waiting for transfers between devices, on_device(): lax.psum_scatter(row_sum, 'col', scatter_dimension=1, tiled=True)  38.3 us
    dot_general x96, matrix products, live_terms(): jnp.dot(portion[7:9], kernel_tile, precision=lax.Precision.HIGHEST)  35.5 us
    another operation x32, loops' own time, slot_terms(): return lax.cond(flag_value > 0, live_terms, empty_terms)  24.6 us
  transfers between devices with their start and end apart: 8, of which 5 were waited for; matrix products, arithmetic and copies ran while one was open for 25% of the time, Pallas kernels for 0%

profile of v1, /device:TPU:0, one launch (start us, length us, event | category | flops | bytes accessed | tf_op | source)
XLA Modules:
  0.0 454.7 jit_solution(4925731637553334860)
XLA Ops:
  6.5 0.7 broadcast_clamp_fusion
  7.2 0.8 maximum_bitcast_fusion.8
  8.3 3.2 scatter_custom_fusion
  12.0 0.8 compare_convert_fusion
  12.8 1.3 add_convert_fusion
  14.1 2.5 collective-permute-start.3
  17.0 0.7 compare_and_fusion
  18.9 38.5 %all_gather.3 = f32[9,4096]{0,1:T(8,128)S(1)} all-gather(f32[9,1024]{0,1:T(8,128)S(1)} %scatter_custom_fusion), channel_id=1, replica_groups=mesh['row'=8,'col'=4] {'col'}, dimensions={1}, use_global_device_ids=true | all-gather | bytes 184320 | tf_op jit(solution)/shard_map/all_gather | solution.py:101
  58.0 1.3 copy.47
  59.3 1.6 gather_fusion
  61.2 1.6 collective-permute-start.1
  63.6 2.7 collective-permute-done.1
  67.0 5.7 %collective-permute-done.2 = f32[9,4096]{1,0:T(8,128)S(1)} collective-permute-done((f32[9,4096]{1,0:T(8,128)S(1)}, f32[9,4096]{1,0:T(8,128)S(1)}, u32[]{:S(2)}, u32[]{:S(2)}) %collective-permute-start.2) | collective-permute-done | bytes 147488 | tf_op jit(solution)/shard_map/ppermute | solution.py:105
  74.9 11.5 %collective-permute-done.4 = f32[18,16,512]{2,1,0:T(8,128)S(1)} collective-permute-done((f32[18,16,512]{2,1,0:T(8,128)S(1)}, f32[18,16,512]{2,1,0:T(8,128)S(1)}, u32[]{:S(2)}, u32[]{:S(2)}) %collective-permute-start.4) | collective-permute-done | bytes 589856 | tf_op jit(solution)/shard_map/ppermute | solution.py:20
  86.9 49.0 %while.34 = (s32[]{:T(128)}, f32[2,2,16,512]{3,1,0,2:T(2,128)S(1)}, f32[16]{0:T(128)S(1)}, f32[18,16,512]{2,0,1:T(8,128)S(1)}, s32[]{:T(128)}, /*index=5*/s32[]{...) while((s32[]{:T(128)}, f32[2,2,16,512]{3,1,0,2:T(2,128)S(1)}, ...), condition=%wide.region_84.85_spmd, body=%wide.region_43.84_spmd.sunk | while | flops 108167224 | bytes 22711308 | solution.py:171
  89.1 4.4 conditional.53
  94.1 4.4 conditional.54
  100.6 4.4 conditional.52
  105.6 4.4 conditional.53
  111.4 4.4 conditional.55
  119.3 4.4 conditional.55
  125.0 4.4 conditional.52
  131.5 4.4 conditional.55
  135.9 39.5 %collective-permute-start.5 = (f32[2,2,16,512]{3,1,0,2:T(2,128)S(1)}, f32[2,2,16,512]{3,1,0,2:T(2,128)S(1)}, u32[]{:S(2)}, u32[]{:S(2)}) collective-permute-start(f32[2,2,16,512]{3,1,0,2:T(2,128)S(1)} %get-tuple-element.1886), channel_id=1, source_target_pairs={{0,16},{16,0},{4,20},{20,4},{8,24},{24,8},{12,28},{28,12},{1,17},{... | collective-permute-start | bytes 393224 | tf_op jit(solution)/shard_map/ppermute | solution.py:20
  175.5 166.8 %while.33 = (s32[]{:T(128)}, f32[2,4096]{1,0:T(2,128)S(1)}, f32[2,8192]{1,0:T(2,128)S(1)}, s32[32]{0:T(128)S(1)}, s32[32]{0:T(128)S(1)}, /*index=5*/s32[32]{0:T(...) while((s32[]{:T(128)}, f32[2,4096]{1,0:T(2,128)S(1)}, ...), condition=%wide.region_42.43_spmd, body=%wide.region_1.42_spmd.sunk | while | flops 108167248 | bytes 22744584 | solution.py:147
  190.9 0.7 fusion.708
  192.2 0.7 fusion.709
  193.5 6.6 %conditional.49 = (f32[2,512]{1,0:T(2,128)S(1)}, f32[2,512]{1,0:T(2,128)S(1)}) conditional(s32[]{:T(128)} %convert_element_type.263, () %tuple.1088, (f32[9,8192]{1,0:T(8,128)S(1)}, s32[]{:T(128)}, f32[9,4096]{1,0:T(8,128)S(1)}, s32[]{:T(128)}, s32[]{:T(128)}, /*index=5*/s32[32]{0:T(128)S(1)}, s32[]{:T(128)}) %tuple.1089), branch_computations={%region_12.12_spmd, %region_13.21_spmd} | conditional | flops 27039756 | bytes 5661272 | solution.py:94
  202.0 8.0 %conditional.48 = (f32[2,512]{1,0:T(2,128)S(1)}, f32[2,512]{1,0:T(2,128)S(1)}) conditional(s32[]{:T(128)} %convert_element_type.262, () %tuple.1086, (f32[9,8192]{1,0:T(8,128)S(1)}, s32[]{:T(128)}, f32[9,4096]{1,0:T(8,128)S(1)}, s32[]{:T(128)}, s32[]{:T(128)}, /*index=5*/s32[32]{0:T(128)S(1)}, s32[]{:T(128)}) %tuple.1087), branch_computations={%region_2.2_spmd, %region_3.11_spmd} | conditional | flops 27039756 | bytes 5661272 | solution.py:94
  211.9 6.7 %conditional.50 = (f32[2,512]{1,0:T(2,128)S(1)}, f32[2,512]{1,0:T(2,128)S(1)}) conditional(s32[]{:T(128)} %convert_element_type.264, () %tuple.1090, (f32[9,8192]{1,0:T(8,128)S(1)}, s32[]{:T(128)}, f32[9,4096]{1,0:T(8,128)S(1)}, s32[]{:T(128)}, s32[]{:T(128)}, /*index=5*/s32[32]{0:T(128)S(1)}, s32[]{:T(128)}) %tuple.1091), branch_computations={%region_22.22_spmd, %region_23.31_spmd} | conditional | flops 27039756 | bytes 5661272 | solution.py:94
  215.2 0.7 dynamic_slice.409
  220.6 6.8 %conditional.51 = (f32[2,512]{1,0:T(2,128)S(1)}, f32[2,512]{1,0:T(2,128)S(1)}) conditional(s32[]{:T(128)} %convert_element_type.265, () %tuple.1092, (f32[9,8192]{1,0:T(8,128)S(1)}, s32[]{:T(128)}, f32[9,4096]{1,0:T(8,128)S(1)}, s32[]{:T(128)}, s32[]{:T(128)}, /*index=5*/s32[32]{0:T(128)S(1)}, s32[]{:T(128)}) %tuple.1093), branch_computations={%region_32.32_spmd, %region_33.41_spmd} | conditional | flops 27039756 | bytes 5661272 | solution.py:94
  223.8 0.7 dynamic_slice.412
  230.0 0.7 fusion.709
  231.3 6.6 %conditional.49 = (f32[2,512]{1,0:T(2,128)S(1)}, f32[2,512]{1,0:T(2,128)S(1)}) conditional(s32[]{:T(128)} %convert_element_type.263, () %tuple.1088, (f32[9,8192]{1,0:T(8,128)S(1)}, s32[]{:T(128)}, f32[9,4096]{1,0:T(8,128)S(1)}, s32[]{:T(128)}, s32[]{:T(128)}, /*index=5*/s32[32]{0:T(128)S(1)}, s32[]{:T(128)}) %tuple.1089), branch_computations={%region_12.12_spmd, %region_13.21_spmd} | conditional | flops 27039756 | bytes 5661272 | solution.py:94
  239.8 8.0 %conditional.48 = (f32[2,512]{1,0:T(2,128)S(1)}, f32[2,512]{1,0:T(2,128)S(1)}) conditional(s32[]{:T(128)} %convert_element_type.262, () %tuple.1086, (f32[9,8192]{1,0:T(8,128)S(1)}, s32[]{:T(128)}, f32[9,4096]{1,0:T(8,128)S(1)}, s32[]{:T(128)}, s32[]{:T(128)}, /*index=5*/s32[32]{0:T(128)S(1)}, s32[]{:T(128)}) %tuple.1087), branch_computations={%region_2.2_spmd, %region_3.11_spmd} | conditional | flops 27039756 | bytes 5661272 | solution.py:94
  249.7 6.7 %conditional.50 = (f32[2,512]{1,0:T(2,128)S(1)}, f32[2,512]{1,0:T(2,128)S(1)}) conditional(s32[]{:T(128)} %convert_element_type.264, () %tuple.1090, (f32[9,8192]{1,0:T(8,128)S(1)}, s32[]{:T(128)}, f32[9,4096]{1,0:T(8,128)S(1)}, s32[]{:T(128)}, s32[]{:T(128)}, /*index=5*/s32[32]{0:T(128)S(1)}, s32[]{:T(128)}) %tuple.1091), branch_computations={%region_22.22_spmd, %region_23.31_spmd} | conditional | flops 27039756 | bytes 5661272 | solution.py:94
  252.9 0.7 dynamic_slice.409
  258.4 8.1 %conditional.51 = (f32[2,512]{1,0:T(2,128)S(1)}, f32[2,512]{1,0:T(2,128)S(1)}) conditional(s32[]{:T(128)} %convert_element_type.265, () %tuple.1092, (f32[9,8192]{1,0:T(8,128)S(1)}, s32[]{:T(128)}, f32[9,4096]{1,0:T(8,128)S(1)}, s32[]{:T(128)}, s32[]{:T(128)}, /*index=5*/s32[32]{0:T(128)S(1)}, s32[]{:T(128)}) %tuple.1093), branch_computations={%region_32.32_spmd, %region_33.41_spmd} | conditional | flops 27039756 | bytes 5661272 | solution.py:94
  263.0 0.7 dynamic_slice.412
  267.8 0.7 fusion.708
  269.1 0.7 fusion.709
  270.4 6.6 %conditional.49 = (f32[2,512]{1,0:T(2,128)S(1)}, f32[2,512]{1,0:T(2,128)S(1)}) conditional(s32[]{:T(128)} %convert_element_type.263, () %tuple.1088, (f32[9,8192]{1,0:T(8,128)S(1)}, s32[]{:T(128)}, f32[9,4096]{1,0:T(8,128)S(1)}, s32[]{:T(128)}, s32[]{:T(128)}, /*index=5*/s32[32]{0:T(128)S(1)}, s32[]{:T(128)}) %tuple.1089), branch_computations={%region_12.12_spmd, %region_13.21_spmd} | conditional | flops 27039756 | bytes 5661272 | solution.py:94
  278.9 8.0 %conditional.48 = (f32[2,512]{1,0:T(2,128)S(1)}, f32[2,512]{1,0:T(2,128)S(1)}) conditional(s32[]{:T(128)} %convert_element_type.262, () %tuple.1086, (f32[9,8192]{1,0:T(8,128)S(1)}, s32[]{:T(128)}, f32[9,4096]{1,0:T(8,128)S(1)}, s32[]{:T(128)}, s32[]{:T(128)}, /*index=5*/s32[32]{0:T(128)S(1)}, s32[]{:T(128)}) %tuple.1087), branch_computations={%region_2.2_spmd, %region_3.11_spmd} | conditional | flops 27039756 | bytes 5661272 | solution.py:94
  288.8 6.7 %conditional.50 = (f32[2,512]{1,0:T(2,128)S(1)}, f32[2,512]{1,0:T(2,128)S(1)}) conditional(s32[]{:T(128)} %convert_element_type.264, () %tuple.1090, (f32[9,8192]{1,0:T(8,128)S(1)}, s32[]{:T(128)}, f32[9,4096]{1,0:T(8,128)S(1)}, s32[]{:T(128)}, s32[]{:T(128)}, /*index=5*/s32[32]{0:T(128)S(1)}, s32[]{:T(128)}) %tuple.1091), branch_computations={%region_22.22_spmd, %region_23.31_spmd} | conditional | flops 27039756 | bytes 5661272 | solution.py:94
  292.1 0.7 dynamic_slice.409
  297.5 8.1 %conditional.51 = (f32[2,512]{1,0:T(2,128)S(1)}, f32[2,512]{1,0:T(2,128)S(1)}) conditional(s32[]{:T(128)} %convert_element_type.265, () %tuple.1092, (f32[9,8192]{1,0:T(8,128)S(1)}, s32[]{:T(128)}, f32[9,4096]{1,0:T(8,128)S(1)}, s32[]{:T(128)}, s32[]{:T(128)}, /*index=5*/s32[32]{0:T(128)S(1)}, s32[]{:T(128)}) %tuple.1093), branch_computations={%region_32.32_spmd, %region_33.41_spmd} | conditional | flops 27039756 | bytes 5661272 | solution.py:94
  302.1 0.7 dynamic_slice.412
  308.3 0.7 fusion.709
  309.6 6.6 %conditional.49 = (f32[2,512]{1,0:T(2,128)S(1)}, f32[2,512]{1,0:T(2,128)S(1)}) conditional(s32[]{:T(128)} %convert_element_type.263, () %tuple.1088, (f32[9,8192]{1,0:T(8,128)S(1)}, s32[]{:T(128)}, f32[9,4096]{1,0:T(8,128)S(1)}, s32[]{:T(128)}, s32[]{:T(128)}, /*index=5*/s32[32]{0:T(128)S(1)}, s32[]{:T(128)}) %tuple.1089), branch_computations={%region_12.12_spmd, %region_13.21_spmd} | conditional | flops 27039756 | bytes 5661272 | solution.py:94
  318.0 6.7 %conditional.48 = (f32[2,512]{1,0:T(2,128)S(1)}, f32[2,512]{1,0:T(2,128)S(1)}) conditional(s32[]{:T(128)} %convert_element_type.262, () %tuple.1086, (f32[9,8192]{1,0:T(8,128)S(1)}, s32[]{:T(128)}, f32[9,4096]{1,0:T(8,128)S(1)}, s32[]{:T(128)}, s32[]{:T(128)}, /*index=5*/s32[32]{0:T(128)S(1)}, s32[]{:T(128)}) %tuple.1087), branch_computations={%region_2.2_spmd, %region_3.11_spmd} | conditional | flops 27039756 | bytes 5661272 | solution.py:94
  326.6 6.7 %conditional.50 = (f32[2,512]{1,0:T(2,128)S(1)}, f32[2,512]{1,0:T(2,128)S(1)}) conditional(s32[]{:T(128)} %convert_element_type.264, () %tuple.1090, (f32[9,8192]{1,0:T(8,128)S(1)}, s32[]{:T(128)}, f32[9,4096]{1,0:T(8,128)S(1)}, s32[]{:T(128)}, s32[]{:T(128)}, /*index=5*/s32[32]{0:T(128)S(1)}, s32[]{:T(128)}) %tuple.1091), branch_computations={%region_22.22_spmd, %region_23.31_spmd} | conditional | flops 27039756 | bytes 5661272 | solution.py:94
  329.9 0.7 dynamic_slice.409
  335.3 6.8 %conditional.51 = (f32[2,512]{1,0:T(2,128)S(1)}, f32[2,512]{1,0:T(2,128)S(1)}) conditional(s32[]{:T(128)} %convert_element_type.265, () %tuple.1092, (f32[9,8192]{1,0:T(8,128)S(1)}, s32[]{:T(128)}, f32[9,4096]{1,0:T(8,128)S(1)}, s32[]{:T(128)}, s32[]{:T(128)}, /*index=5*/s32[32]{0:T(128)S(1)}, s32[]{:T(128)}) %tuple.1093), branch_computations={%region_32.32_spmd, %region_33.41_spmd} | conditional | flops 27039756 | bytes 5661272 | solution.py:94
  338.5 0.7 dynamic_slice.412
  342.4 1.2 scatter_fusion
  343.6 2.0 copy.58
  345.7 1.2 scatter_fusion.1
  346.9 2.7 copy.59
  349.6 0.7 copy-done.1
  350.3 38.3 %reduce-scatter.3.cloned.1.call-done = f32[2,1024]{0,1:T(8,128)} async-done(((f32[2,4096]{0,1:T(8,128)}), f32[2,1024]{0,1:T(8,128)}) %reduce-scatter.3.cloned.1.call-update) | async-done | bytes 8208 | tf_op jit(solution)/shard_map/reduce_scatter | solution.py:187
  388.7 53.8 %reduce-scatter.5.cloned.1.call-done = f32[2,1024]{0,1:T(8,128)} async-done(((f32[2,8192]{0,1:T(8,128)}), f32[2,1024]{0,1:T(8,128)}) %reduce-scatter.5.cloned.1.call-update) | async-done | bytes 8208 | tf_op jit(solution)/shard_map/reduce_scatter | solution.py:187
  442.4 1.3 add.6301
  443.7 2.8 gather_fusion.2
  (895 shorter events, 159.4 us)
Async XLA Ops:
  6.5 10.5 %copy-start.6 = (s32[32,2]{0,1:T(2,128)S(1)}, s32[32,2]{0,1:T(2,128)}, u32[]{:S(2)}) copy-start(s32[32,2]{0,1:T(2,128)} %param.98) | copy-start | bytes 772
  6.5 382.1 %reduce-scatter.3.cloned.1.call-start = ((), (), s32[]{:S(2)}) async-start(), calls=%async_computation.2 | async-start | bytes 2621440 | tf_op jit(solution)/shard_map/reduce_scatter | solution.py:187
  11.5 49.5 %collective-permute-start = (f32[9,1024]{0,1:T(8,128)S(1)}, f32[9,1024]{0,1:T(8,128)S(1)}, u32[]{:S(2)}, u32[]{:S(2)}) collective-permute-start(f32[9,1024]{0,1:T(8,128)S(1)} %scatter_custom_fusion), channel_id=1, source_target_pairs={{0,4},{4,0},{8,12},{12,8},{16,20},{20,16},{24,28},{28,24},{1,5},{5... | collective-permute-start | bytes 110600 | tf_op jit(solution)/shard_map/ppermute | solution.py:105
  12.8 4.9 %copy-start.9 = (s32[32]{0:T(128)}, s32[32]{0:T(128)S(1)}, u32[]{:S(2)}) copy-start(s32[32]{0:T(128)S(1)} %compare_convert_fusion) | copy-start | bytes 388
  14.1 72.7 %collective-permute-start.3 = (f32[16]{0:T(128)}, f32[16]{0:T(128)S(1)}, u32[]{:S(2)}, u32[]{:S(2)}) collective-permute-start(f32[16]{0:T(128)} %add_convert_fusion), channel_id=1, source_target_pairs={{0,16},{16,0},{4,20},{20,4},{8,24},{24,8},{12,28},{28,12},{1,17},{... | collective-permute-start | bytes 200 | tf_op jit(solution)/shard_map/ppermute | solution.py:20
  18.3 0.6 copy-start.4
  61.2 5.0 %collective-permute-start.1 = (f32[9,2048]{1,0:T(8,128)S(1)}, f32[9,2048]{1,0:T(8,128)S(1)}, u32[]{:S(2)}, u32[]{:S(2)}) collective-permute-start(f32[9,2048]{1,0:T(8,128)S(1)} %maximum_select_fusion.4), channel_id=1, source_target_pairs={{0,8},{4,12},{8,0},{12,4},{16,24},{20,28},{24,16},{28,20},{1,9},{5... | collective-permute-start | bytes 221192 | tf_op jit(solution)/shard_map/ppermute | solution.py:105
  66.3 7.4 %copy-start.7 = (pred[16]{0:T(512)(128)(4,1)S(1)}, pred[16]{0:T(512)(128)(4,1)}, u32[]{:S(2)}) copy-start(pred[16]{0:T(512)(128)(4,1)} %get-tuple-element.1962) | copy-start | bytes 52
  66.3 7.4 %copy-start.8 = (pred[16]{0:T(512)(128)(4,1)S(1)}, pred[16]{0:T(512)(128)(4,1)}, u32[]{:S(2)}) copy-start(pred[16]{0:T(512)(128)(4,1)} %get-tuple-element.1960) | copy-start | bytes 52
  66.3 6.4 %collective-permute-start.2 = (f32[9,4096]{1,0:T(8,128)S(1)}, f32[9,4096]{1,0:T(8,128)S(1)}, u32[]{:S(2)}, u32[]{:S(2)}) collective-permute-start(f32[9,4096]{1,0:T(8,128)S(1)} %maximum_select_fusion.2), channel_id=1, source_target_pairs={{0,16},{4,20},{8,24},{12,28},{16,0},{20,4},{24,8},{28,12},{1,17},{... | collective-permute-start | bytes 442376 | tf_op jit(solution)/shard_map/ppermute | solution.py:105
  74.3 12.2 %collective-permute-start.4 = (f32[18,16,512]{2,1,0:T(8,128)S(1)}, f32[18,16,512]{2,1,0:T(8,128)S(1)}, u32[]{:S(2)}, u32[]{:S(2)}) collective-permute-start(f32[18,16,512]{2,1,0:T(8,128)S(1)} %copy.56), channel_id=1, source_target_pairs={{0,16},{16,0},{4,20},{20,4},{8,24},{24,8},{12,28},{28,12},{1,17},{... | collective-permute-start | bytes 1769480 | tf_op jit(solution)/shard_map/ppermute | solution.py:20
  86.9 88.6 %copy-start = (s32[32]{0:T(128)S(1)}, s32[32]{0:T(128)}, u32[]{:S(2)}) copy-start(s32[32]{0:T(128)} %param.99) | copy-start | bytes 388
  86.9 88.6 %copy-start.10 = (s32[32]{0:T(128)S(1)}, s32[32]{0:T(128)}, u32[]{:S(2)}) copy-start(s32[32]{0:T(128)} %copy-done.9) | copy-start | bytes 388
  135.9 206.5 %collective-permute-start.5 = (f32[2,2,16,512]{3,1,0,2:T(2,128)S(1)}, f32[2,2,16,512]{3,1,0,2:T(2,128)S(1)}, u32[]{:S(2)}, u32[]{:S(2)}) collective-permute-start(f32[2,2,16,512]{3,1,0,2:T(2,128)S(1)} %get-tuple-element.1886), channel_id=1, source_target_pairs={{0,16},{16,0},{4,20},{20,4},{8,24},{24,8},{12,28},{28,12},{1,17},{... | collective-permute-start | bytes 393224 | tf_op jit(solution)/shard_map/ppermute | solution.py:20
  175.5 166.9 %copy-start.5 = (s32[16]{0:T(128)S(1)}, s32[16]{0:T(128)}, u32[]{:S(2)}) copy-start(s32[16]{0:T(128)} %copy-done.4) | copy-start | bytes 196
  343.6 2.1 copy-start.3
  345.6 96.8 %reduce-scatter.5.cloned.1.call-start = ((), (), s32[]{:S(2)}) async-start(), calls=%async_computation.3 | async-start | bytes 4718592 | tf_op jit(solution)/shard_map/reduce_scatter | solution.py:187
  349.6 0.7 copy-start.1
  350.3 96.7 %copy-start.2 = (f32[1024]{0:T(1024)S(1)}, f32[1024]{0:T(1024)}, u32[]{:S(2)}) copy-start(f32[1024]{0:T(1024)} %param.96) | copy-start | bytes 12292
Sparse Core Ops, SparseCore 0:
  345.8 42.8 reduce-scatter.2
  392.0 50.3 reduce-scatter.4
